TPU v7x, 32 devices: a whole 2x2x4 slice. The times are simulated.
32 devices in a mesh: pts: 4 (over x, core), snap: 8 (over z, y).
Axes of the slice: x: 2, y: 2, z: 4, core: 2. Of those that a mesh axis runs over, the one named last changes fastest.
Arguments:
- snapshots: float32 [4096, 8192], P('pts', 'snap'), may hold values from -8 to 8
- modes_init: float32 [4096, 128], P('pts'), may hold values from -6 to 6
- coefs_init: float32 [128, 8192], P(None, 'snap'), may hold values from -0.09375 to 0.09375
Outputs:
- modes: float32 [4096, 128], P('pts')
- amplitudes: float32 [128, 8192], P(None, 'snap')
All inputs are finite; a program needn't handle non-finite values.
Results may differ from a plain program's by a relative error of at most 0.0003.
Values sent between devices are 32-bit elements; how exact they have to be, the bound alone decides.
A program may use at most 64 MiB of HBM per device.

v0:
```python
import jax
import jax.numpy as jnp
from jax import lax
from jax.sharding import PartitionSpec as P

OUTER = 2
INNER = 2
HUBER = 1.345
RIDGE = 0.01


def high_dot(left, right):
    return jnp.dot(left, right, preferred_element_type=jnp.float32, precision=lax.Precision.HIGHEST)


def clipped_error(snapshots, modes, coefs, count):
    error = snapshots - high_dot(modes, coefs)
    total = lax.psum(jnp.sum(error * error), ("pts", "snap"))
    limit = HUBER * jnp.sqrt(total / count + 1e-06)
    return jnp.clip(error, -limit, limit)


def shards(snapshots, modes_init, coefs_init):
    modes = modes_init
    coefs = coefs_init
    rows, width = snapshots.shape
    points = rows * lax.axis_size("pts")
    count = float(points * width * lax.axis_size("snap"))
    rank = modes.shape[1]
    eye = jnp.eye(rank, dtype=jnp.float32)
    for outer in range(OUTER):
        gram = lax.psum(high_dot(modes.T, modes), "pts") + RIDGE * eye
        factor = jnp.linalg.cholesky(gram)
        for inner in range(INNER):
            clipped = clipped_error(snapshots, modes, coefs, count)
            product = high_dot(modes.T, clipped)
            share = lax.psum_scatter(product, "pts", scatter_dimension=1, tiled=True)
            span = share.shape[1]
            own = lax.dynamic_slice_in_dim(coefs, lax.axis_index("pts") * span, span, 1)
            own = own + jax.scipy.linalg.cho_solve((factor, True), share)
            coefs = lax.all_gather(own, "pts", axis=1, tiled=True)
        clipped = clipped_error(snapshots, modes, coefs, count)
        hess = lax.psum(high_dot(coefs, coefs.T), "snap") + RIDGE * eye
        hfactor = jnp.linalg.cholesky(hess)
        moment = high_dot(clipped, coefs.T)
        summed = lax.psum(moment, "snap")
        modes = modes + jax.scipy.linalg.cho_solve((hfactor, True), summed.T).T
    return (modes, coefs * jnp.sqrt(jnp.float32(points)))


def solution(mesh):
    in_specs = (P("pts", "snap"), P("pts", None), P(None, "snap"))
    out_specs = (P("pts", None), P(None, "snap"))
    return jax.shard_map(shards, mesh=mesh, in_specs=in_specs, out_specs=out_specs, check_vma=False)
```

profile of v0, /device:TPU:0, one launch (start us, length us, event | category | flops | bytes accessed | tf_op | source)
XLA Modules:
  0.0 692.1 jit_solution(7492501816023668363)
XLA Ops:
  7.2 2.8 fusion.66
  10.1 8.6 %multiply_reduce_fusion.5 = (f32[]{:T(128)}, f32[1024,1024]{1,0:T(8,128)}) fusion(f32[1024,1024]{1,0:T(8,128)} %param.8, f32[1024,128]{1,0:T(8,128)} %param.9, f32[128,1024]{1,0:T(8,128)} %param.10), kind=kOutput, calls=%fused_computation.25 | convolution fusion | flops 1613758464 | bytes 9437188 | tf_op jit(solution)/shard_map/dot_general | solution.py:13
  18.8 42.5 %psum.85 = f32[]{:T(128)} all-reduce(f32[]{:T(128)} %get-tuple-element.11), channel_id=1, replica_groups=mesh['pts'=4,'snap'=8] {'pts','snap'}, use_global_device_ids=true, to_apply=%region_4.6 | all-reduce | flops 1 | bytes 8 | tf_op jit(solution)/shard_map/psum | solution.py:18
  61.9 9.6 %fusion.32 = f32[128,1024]{0,1:T(8,128)} fusion(f32[1024,128]{1,0:T(8,128)S(1)} %copy-done, f32[1024,1024]{1,0:T(8,128)} %get-tuple-element.12, f32[]{:T(128)S(6)} %neg.18, f32[]{:T(128)S(6)} %mul.63), kind=kOutput, calls=%fused_computation.46 | convolution fusion | flops 1612709888 | bytes 5242888 | tf_op jit(solution)/shard_map/dot_general | solution.py:13
  72.2 5.4 copy.7
  77.5 0.9 select_add_fusion.3
  78.5 0.9 fusion.63
  79.4 11.7 %cholesky.74 = f32[128,128]{1,0:T(8,128)S(1)} custom-call(f32[128,128]{1,0:T(8,128)S(1)} %fusion.63), custom_call_target="Cholesky" | custom-call | tf_op jit(solution)/shard_map/jit(cholesky)/cholesky | solution.py:33
  91.1 0.6 compare_reduce_fusion.3
  91.8 0.7 fusion.38
  92.4 9.8 %custom-call.16 = f32[1,128,128]{1,2,0:T(8,128)S(1)} custom-call(f32[1,128,128]{2,1,0:T(8,128)S(1)} %fusion.38), custom_call_target="InvertDiagBlocksLowerTriangular" | custom-call | tf_op jit(solution)/shard_map/jit(_cho_solve)/triangular_solve | solution.py:40
  102.3 1.2 fusion.61
  103.5 1.2 convolution_add_fusion.3
  104.7 8.0 %all_gather.12 = f32[128,1024]{1,0:T(8,128)S(1)} all-gather(f32[128,256]{1,0:T(8,128)S(1)} %convolution_add_fusion.3), channel_id=1, replica_groups=mesh['pts'=4,'snap'=8] {'pts'}, dimensions={1}, use_global_device_ids=true | all-gather | bytes 655360 | tf_op jit(solution)/shard_map/all_gather | solution.py:41
  112.6 7.7 %multiply_reduce_fusion.4 = (f32[]{:T(128)}, f32[1024,1024]{0,1:T(8,128)}) fusion(f32[1024,1024]{0,1:T(8,128)} %copy.7, f32[128,1024]{1,0:T(8,128)S(1)} %all_gather.12, f32[1024,128]{1,0:T(8,128)S(1)} %copy-done), kind=kOutput, calls=%fused_computation.21 | convolution fusion | flops 1613758464 | bytes 9437188 | tf_op jit(solution)/shard_map/dot_general | solution.py:13
  120.3 39.7 %psum.86 = f32[]{:T(128)} all-reduce(f32[]{:T(128)} %get-tuple-element.13), channel_id=1, replica_groups=mesh['pts'=4,'snap'=8] {'pts','snap'}, use_global_device_ids=true, to_apply=%region_7.10 | all-reduce | flops 1 | bytes 8 | tf_op jit(solution)/shard_map/psum | solution.py:18
  160.7 6.4 fusion.35
  167.2 22.0 %reduce-scatter.7.cloned.1.call-done = f32[128,256]{0,1:T(8,128)} async-done(((f32[128,1024]{0,1:T(8,128)}), f32[128,256]{0,1:T(8,128)}) %reduce-scatter.7.cloned.1.call-update) | async-done | bytes 131088 | tf_op jit(solution)/shard_map/reduce_scatter | solution.py:37
  189.2 1.2 fusion.58
  190.7 6.6 all_gather.13
  197.3 7.6 %multiply_reduce_fusion.3 = (f32[]{:T(128)}, f32[1024,1024]{0,1:T(8,128)}) fusion(f32[1024,1024]{0,1:T(8,128)} %copy.7, f32[128,1024]{1,0:T(8,128)S(1)} %all_gather.13, f32[1024,128]{1,0:T(8,128)S(1)} %copy-done), kind=kOutput, calls=%fused_computation.17 | convolution fusion | flops 1613758464 | bytes 9437188 | tf_op jit(solution)/shard_map/dot_general | solution.py:13
  204.9 1.2 fusion.67
  206.1 40.0 %psum.88 = f32[]{:T(128)} all-reduce(f32[]{:T(128)} %get-tuple-element.15), channel_id=1, replica_groups=mesh['pts'=4,'snap'=8] {'pts','snap'}, use_global_device_ids=true, to_apply=%region_11.14 | all-reduce | flops 1 | bytes 8 | tf_op jit(solution)/shard_map/psum | solution.py:18
  246.8 5.7 fusion.9
  253.0 73.4 %all-reduce.13.cloned.1.call-done = (f32[128,1024]{1,0:T(8,128)}, f32[128,128]{0,1:T(8,128)}) async-done(((f32[128,1024]{1,0:T(8,128)}, f32[128,128]{0,1:T(8,128)}), (f32[128,1024]{1,0:T(8,128)}, f32[128,128]{0,1:T(8,128)})) %all-reduce.13.cloned.1.call-update) | async-done | bytes 589840 | tf_op jit(solution)/shard_map/psum | solution.py:46
  326.4 0.9 select_add_fusion.2
  327.4 0.9 fusion.56
  328.2 11.7 %cholesky.85 = f32[128,128]{1,0:T(8,128)S(1)} custom-call(f32[128,128]{1,0:T(8,128)S(1)} %fusion.56), custom_call_target="Cholesky" | custom-call | tf_op jit(solution)/shard_map/jit(cholesky)/cholesky | solution.py:44
  340.0 0.6 compare_reduce_fusion.2
  340.6 0.7 fusion.39
  341.3 9.8 %custom-call.18 = f32[1,128,128]{1,2,0:T(8,128)S(1)} custom-call(f32[1,128,128]{2,1,0:T(8,128)S(1)} %fusion.39), custom_call_target="InvertDiagBlocksLowerTriangular" | custom-call | tf_op jit(solution)/shard_map/jit(_cho_solve)/triangular_solve | solution.py:47
  351.1 1.7 fusion.54
  353.4 1.2 fusion.68
  354.6 7.6 %multiply_reduce_fusion.2 = (f32[]{:T(128)}, f32[1024,1024]{1,0:T(8,128)}) fusion(f32[1024,1024]{1,0:T(8,128)} %param.8, f32[1024,128]{0,1:T(8,128)S(1)} %fusion.30, f32[128,1024]{1,0:T(8,128)S(1)} %all_gather.13), kind=kOutput, calls=%fused_computation.13 | convolution fusion | flops 1613758464 | bytes 9437188 | tf_op jit(solution)/shard_map/dot_general | solution.py:13
  362.2 40.0 %psum.91 = f32[]{:T(128)} all-reduce(f32[]{:T(128)} %get-tuple-element.17), channel_id=1, replica_groups=mesh['pts'=4,'snap'=8] {'pts','snap'}, use_global_device_ids=true, to_apply=%region_15.19 | all-reduce | flops 1 | bytes 8 | tf_op jit(solution)/shard_map/psum | solution.py:18
  402.9 5.7 fusion.6
  408.7 0.9 select_add_fusion.1
  409.7 0.9 fusion.52
  410.5 11.7 %cholesky.96 = f32[128,128]{1,0:T(8,128)S(1)} custom-call(f32[128,128]{1,0:T(8,128)S(1)} %fusion.52), custom_call_target="Cholesky" | custom-call | tf_op jit(solution)/shard_map/jit(cholesky)/cholesky | solution.py:33
  422.3 0.6 compare_reduce_fusion.1
  422.9 0.7 fusion.40
  423.6 9.8 %custom-call.19 = f32[1,128,128]{1,2,0:T(8,128)S(1)} custom-call(f32[1,128,128]{2,1,0:T(8,128)S(1)} %fusion.40), custom_call_target="InvertDiagBlocksLowerTriangular" | custom-call | tf_op jit(solution)/shard_map/jit(_cho_solve)/triangular_solve | solution.py:40
  433.4 1.2 fusion.50
  434.9 8.1 %all_gather.14 = f32[128,1024]{1,0:T(8,128)S(1)} all-gather(f32[128,256]{1,0:T(8,128)S(1)} %convolution_add_fusion.1), channel_id=1, replica_groups=mesh['pts'=4,'snap'=8] {'pts'}, dimensions={1}, use_global_device_ids=true | all-gather | bytes 655360 | tf_op jit(solution)/shard_map/all_gather | solution.py:41
  443.1 7.6 %multiply_reduce_fusion.1 = (f32[]{:T(128)}, f32[1024,1024]{1,0:T(8,128)}) fusion(f32[1024,1024]{1,0:T(8,128)} %param.8, f32[1024,128]{0,1:T(8,128)S(1)} %fusion.30, f32[128,1024]{1,0:T(8,128)S(1)} %all_gather.14), kind=kOutput, calls=%fused_computation.9 | convolution fusion | flops 1613758464 | bytes 9437188 | tf_op jit(solution)/shard_map/dot_general | solution.py:13
  450.6 38.7 %psum.92 = f32[]{:T(128)} all-reduce(f32[]{:T(128)} %get-tuple-element.19), channel_id=1, replica_groups=mesh['pts'=4,'snap'=8] {'pts','snap'}, use_global_device_ids=true, to_apply=%region_18.22 | all-reduce | flops 1 | bytes 8 | tf_op jit(solution)/shard_map/psum | solution.py:18
  490.1 5.7 fusion.3
  495.8 22.3 %reduce-scatter.11.cloned.1.call-done = f32[128,256]{1,0:T(8,128)} async-done(((f32[128,1024]{1,0:T(8,128)}), f32[128,256]{1,0:T(8,128)}) %reduce-scatter.11.cloned.1.call-update) | async-done | bytes 131088 | tf_op jit(solution)/shard_map/reduce_scatter | solution.py:37
  518.2 1.2 fusion.47
  519.6 6.6 all_gather.15
  526.2 7.6 %multiply_reduce_fusion = (f32[]{:T(128)}, f32[1024,1024]{1,0:T(8,128)}) fusion(f32[1024,1024]{1,0:T(8,128)} %param.8, f32[1024,128]{0,1:T(8,128)S(1)} %fusion.30, f32[128,1024]{1,0:T(8,128)S(1)} %all_gather.15), kind=kOutput, calls=%fused_computation.5 | convolution fusion | flops 1613758464 | bytes 9437188 | tf_op jit(solution)/shard_map/dot_general | solution.py:13
  533.8 1.2 fusion.69
  535.0 40.2 %psum.94 = f32[]{:T(128)} all-reduce(f32[]{:T(128)} %get-tuple-element.21), channel_id=1, replica_groups=mesh['pts'=4,'snap'=8] {'pts','snap'}, use_global_device_ids=true, to_apply=%region_22.26 | all-reduce | flops 1 | bytes 8 | tf_op jit(solution)/shard_map/psum | solution.py:18
  575.9 7.3 %fusion = f32[128,1024]{1,0:T(8,128)} fusion(f32[128,1024]{1,0:T(8,128)S(1)} %all_gather.15, f32[1024,1024]{1,0:T(8,128)} %get-tuple-element.22, f32[]{:T(128)S(6)} %neg.23, f32[]{:T(128)S(6)} %mul.73), kind=kOutput, calls=%fused_computation.2 | convolution fusion | flops 1612709888 | bytes 5242888 | tf_op jit(solution)/shard_map/dot_general | solution.py:13
  583.3 0.8 broadcast_multiply_fusion
  584.1 73.0 %all-reduce.11.cloned.1.call-done = (f32[128,1024]{1,0:T(8,128)}, f32[128,128]{0,1:T(8,128)}) async-done(((f32[128,1024]{1,0:T(8,128)}, f32[128,128]{0,1:T(8,128)}), (f32[128,1024]{1,0:T(8,128)}, f32[128,128]{0,1:T(8,128)})) %all-reduce.11.cloned.1.call-update) | async-done | bytes 589840 | tf_op jit(solution)/shard_map/psum | solution.py:46
  657.1 0.9 select_add_fusion
  658.1 0.9 fusion.45
  658.9 11.7 %cholesky.107 = f32[128,128]{1,0:T(8,128)S(1)} custom-call(f32[128,128]{1,0:T(8,128)S(1)} %fusion.45), custom_call_target="Cholesky" | custom-call | tf_op jit(solution)/shard_map/jit(cholesky)/cholesky | solution.py:44
  670.7 0.6 compare_reduce_fusion
  671.3 0.7 fusion.41
  672.0 9.8 %custom-call.21 = f32[1,128,128]{1,2,0:T(8,128)S(1)} custom-call(f32[1,128,128]{2,1,0:T(8,128)S(1)} %fusion.41), custom_call_target="InvertDiagBlocksLowerTriangular" | custom-call | tf_op jit(solution)/shard_map/jit(_cho_solve)/triangular_solve | solution.py:47
  681.8 1.7 fusion.43
  684.1 1.0 copy.16
  (36 shorter events, 3.9 us)
Async XLA Ops:
  7.2 70.4 %all-reduce.7.cloned.1.call-start = ((), (), s32[]{:S(2)}) async-start(), calls=%async_computation.4 | async-start | bytes 131072 | tf_op jit(solution)/shard_map/psum | solution.py:32
  10.1 51.9 %copy-start = (f32[1024,128]{1,0:T(8,128)S(1)}, f32[1024,128]{1,0:T(8,128)}, u32[]{:S(2)}) copy-start(f32[1024,128]{1,0:T(8,128)} %param.9) | copy-start | bytes 1572868
  10.1 92.2 %reduce-scatter.5.cloned.1.call-start = ((), (), s32[]{:S(2)}) async-start(), calls=%async_computation.5 | async-start | bytes 655360 | tf_op jit(solution)/shard_map/reduce_scatter | solution.py:37
  71.6 117.6 %reduce-scatter.7.cloned.1.call-start = ((), (), s32[]{:S(2)}) async-start(), calls=%async_computation.6 | async-start | bytes 655360 | tf_op jit(solution)/shard_map/reduce_scatter | solution.py:37
  167.1 159.3 %all-reduce.13.cloned.1.call-start = ((), (), s32[]{:S(2)}) async-start(), calls=%async_computation.11 | async-start | bytes 1179648 | tf_op jit(solution)/shard_map/psum | solution.py:46
  252.5 156.2 %all-reduce.9.cloned.1.call-start = ((), (), s32[]{:S(2)}) async-start(), calls=%async_computation.7 | async-start | bytes 131072 | tf_op jit(solution)/shard_map/psum | solution.py:32
  362.2 71.2 %reduce-scatter.9.cloned.1.call-start = ((), (), s32[]{:S(2)}) async-start(), calls=%async_computation.8 | async-start | bytes 655360 | tf_op jit(solution)/shard_map/reduce_scatter | solution.py:37
  408.6 109.5 %reduce-scatter.11.cloned.1.call-start = ((), (), s32[]{:S(2)}) async-start(), calls=%async_computation.9 | async-start | bytes 655360 | tf_op jit(solution)/shard_map/reduce_scatter | solution.py:37
  495.8 161.4 %all-reduce.11.cloned.1.call-start = ((), (), s32[]{:S(2)}) async-start(), calls=%async_computation.10 | async-start | bytes 1179648 | tf_op jit(solution)/shard_map/psum | solution.py:46
Sparse Core Ops, SparseCore 0:
  10.9 34.2 all-reduce.6
  71.7 21.8 reduce-scatter.4
  167.3 21.8 reduce-scatter.6
  252.7 73.7 all-reduce.12
  362.3 30.6 all-reduce.8
  408.8 21.6 reduce-scatter.8
  495.9 22.2 reduce-scatter.10
  583.4 73.6 all-reduce.10
where the time goes:
time: 698 us; the launch traced here: 692 us
  blocking collectives  270 us (39%)
  waiting for transfers between devices  191 us (27%)
  matrix products  105 us (15%)
  other arithmetic  99.1 us (14%)
  between operations  18.8 us (3%)
    psum x6, blocking collectives, clipped_error(): total = lax.psum(jnp.sum(error * error), ('pts', 'snap'))  241 us
    psum x2, waiting for transfers between devices, shards(): summed = lax.psum(moment, 'snap')  146 us
    dot_general x16, matrix products, high_dot(): jnp.dot(left, right, preferred_element_type=jnp.float32, precision=lax.Pr...  93.5 us
    reduce_scatter x4, waiting for transfers between devices, shards(): share = lax.psum_scatter(product, 'pts', scatter_dimension=1, tiled=True)  44.4 us
    all_gather x4, blocking collectives, shards(): coefs = lax.all_gather(own, 'pts', axis=1, tiled=True)  29.3 us
    another operation x6, other arithmetic, shards(): factor = jnp.linalg.cholesky(gram)  24.8 us
    another operation x6, other arithmetic, shards(): hfactor = jnp.linalg.cholesky(hess)  24.8 us
    another operation x4, other arithmetic, shards(): own = own + jax.scipy.linalg.cho_solve((factor, True), share)  20.9 us
  transfers between devices with their start and end apart: 8, of which 4 were waited for; matrix products, arithmetic and copies ran while one was open for 12% of the time, Pallas kernels for 0%

commit v1 on v0

--- a/solution.py
+++ b/solution.py
@@ -43,7 +43,9 @@
         hess = lax.psum(high_dot(coefs, coefs.T), "snap") + RIDGE * eye
         hfactor = jnp.linalg.cholesky(hess)
         moment = high_dot(clipped, coefs.T)
-        summed = lax.psum(moment, "snap")
+        summed = moment
+        for hop in (1, 2, 4):
+            summed = summed + lax.ppermute(summed, "snap", [(dev, dev ^ hop) for dev in range(8)])
         modes = modes + jax.scipy.linalg.cho_solve((hfactor, True), summed.T).T
     return (modes, coefs * jnp.sqrt(jnp.float32(points)))
 

time: 698 us -> 720 us (1.032)
  starting transfers between devices: 1.07 us -> 12.8 us
  waiting for transfers between devices: 191 us -> 202 us
    ppermute x0 -> x6, waiting for transfers between devices: none -> 21.2 us  [shards(): lax.ppermute(summed, 'snap', [(dev, dev ^ hop) for dev in range(8)])]
    ppermute x0 -> x6, starting transfers between devices: none -> 11.8 us  [shards(): lax.ppermute(summed, 'snap', [(dev, dev ^ hop) for dev in range(8)])]
    psum x2, waiting for transfers between devices: 146 us -> 137 us  [shards(): hess = lax.psum(high_dot(coefs, coefs.T), 'snap') + RIDGE * eye]
  transfers between devices with their start and end apart: 8 -> 14, of which waited for: 4 -> 6; matrix products, arithmetic and copies ran while one was open for 12% -> 18% of each run, Pallas kernels for 0% -> 0%
where the time goes in v1:
time: 720 us; the launch traced here: 715 us
  blocking collectives  271 us (38%)
  waiting for transfers between devices  202 us (28%)
  matrix products  103 us (14%)
  other arithmetic  99.3 us (14%)
  between operations  18.9 us (3%)
  starting transfers between devices  12.8 us (2%)
    psum x6, blocking collectives, clipped_error(): total = lax.psum(jnp.sum(error * error), ('pts', 'snap'))  242 us
    psum x2, waiting for transfers between devices, shards(): hess = lax.psum(high_dot(coefs, coefs.T), 'snap') + RIDGE * eye  137 us
    dot_general x16, matrix products, high_dot(): jnp.dot(left, right, preferred_element_type=jnp.float32, precision=lax.Pr...  94.2 us
    reduce_scatter x4, waiting for transfers between devices, shards(): share = lax.psum_scatter(product, 'pts', scatter_dimension=1, tiled=True)  44 us
    all_gather x4, blocking collectives, shards(): coefs = lax.all_gather(own, 'pts', axis=1, tiled=True)  29.3 us
    another operation x6, other arithmetic, shards(): factor = jnp.linalg.cholesky(gram)  24.8 us
    another operation x6, other arithmetic, shards(): hfactor = jnp.linalg.cholesky(hess)  24.8 us
    ppermute x6, waiting for transfers between devices, shards(): lax.ppermute(summed, 'snap', [(dev, dev ^ hop) for dev in range(8)])  21.2 us
  transfers between devices with their start and end apart: 14, of which 6 were waited for; matrix products, arithmetic and copies ran while one was open for 18% of the time, Pallas kernels for 0%

profile of v1, /device:TPU:0, one launch (start us, length us, event | category | flops | bytes accessed | tf_op | source)
XLA Modules:
  0.0 714.8 jit_solution(13857297258475927996)
XLA Ops:
  7.2 2.8 fusion.70
  10.1 8.6 %multiply_reduce_fusion.5 = (f32[]{:T(128)}, f32[1024,1024]{1,0:T(8,128)}) fusion(f32[1024,1024]{1,0:T(8,128)} %param.8, f32[1024,128]{1,0:T(8,128)} %param.9, f32[128,1024]{1,0:T(8,128)} %param.10), kind=kOutput, calls=%fused_computation.25 | convolution fusion | flops 1613758464 | bytes 9437188 | tf_op jit(solution)/shard_map/dot_general | solution.py:13
  18.8 42.5 %psum.71 = f32[]{:T(128)} all-reduce(f32[]{:T(128)} %get-tuple-element.7), channel_id=1, replica_groups=mesh['pts'=4,'snap'=8] {'pts','snap'}, use_global_device_ids=true, to_apply=%region_4.6 | all-reduce | flops 1 | bytes 8 | tf_op jit(solution)/shard_map/psum | solution.py:18
  61.9 9.6 %fusion.32 = f32[128,1024]{0,1:T(8,128)} fusion(f32[1024,128]{1,0:T(8,128)S(1)} %copy-done, f32[1024,1024]{1,0:T(8,128)} %get-tuple-element.8, f32[]{:T(128)S(6)} %neg.18, f32[]{:T(128)S(6)} %mul.63), kind=kOutput, calls=%fused_computation.46 | convolution fusion | flops 1612709888 | bytes 5242888 | tf_op jit(solution)/shard_map/dot_general | solution.py:13
  72.2 5.4 copy.7
  77.5 0.9 select_add_fusion.3
  78.5 0.9 fusion.67
  79.4 11.7 %cholesky.74 = f32[128,128]{1,0:T(8,128)S(1)} custom-call(f32[128,128]{1,0:T(8,128)S(1)} %fusion.67), custom_call_target="Cholesky" | custom-call | tf_op jit(solution)/shard_map/jit(cholesky)/cholesky | solution.py:33
  91.7 0.7 fusion.44
  92.4 9.8 %custom-call.16 = f32[1,128,128]{1,2,0:T(8,128)S(1)} custom-call(f32[1,128,128]{2,1,0:T(8,128)S(1)} %fusion.44), custom_call_target="InvertDiagBlocksLowerTriangular" | custom-call | tf_op jit(solution)/shard_map/jit(_cho_solve)/triangular_solve | solution.py:40
  102.3 1.2 fusion.65
  103.5 1.2 convolution_add_fusion.3
  104.7 8.0 %all_gather.12 = f32[128,1024]{1,0:T(8,128)S(1)} all-gather(f32[128,256]{1,0:T(8,128)S(1)} %convolution_add_fusion.3), channel_id=1, replica_groups=mesh['pts'=4,'snap'=8] {'pts'}, dimensions={1}, use_global_device_ids=true | all-gather | bytes 655360 | tf_op jit(solution)/shard_map/all_gather | solution.py:41
  112.6 7.7 %multiply_reduce_fusion.4 = (f32[]{:T(128)}, f32[1024,1024]{0,1:T(8,128)}) fusion(f32[1024,1024]{0,1:T(8,128)} %copy.7, f32[128,1024]{1,0:T(8,128)S(1)} %all_gather.12, f32[1024,128]{1,0:T(8,128)S(1)} %copy-done), kind=kOutput, calls=%fused_computation.21 | convolution fusion | flops 1613758464 | bytes 9437188 | tf_op jit(solution)/shard_map/dot_general | solution.py:13
  120.3 39.7 %psum.72 = f32[]{:T(128)} all-reduce(f32[]{:T(128)} %get-tuple-element.9), channel_id=1, replica_groups=mesh['pts'=4,'snap'=8] {'pts','snap'}, use_global_device_ids=true, to_apply=%region_7.10 | all-reduce | flops 1 | bytes 8 | tf_op jit(solution)/shard_map/psum | solution.py:18
  160.7 6.4 fusion.35
  167.2 22.0 %reduce-scatter.7.cloned.1.call-done = f32[128,256]{0,1:T(8,128)} async-done(((f32[128,1024]{0,1:T(8,128)}), f32[128,256]{0,1:T(8,128)}) %reduce-scatter.7.cloned.1.call-update) | async-done | bytes 131088 | tf_op jit(solution)/shard_map/reduce_scatter | solution.py:37
  189.2 1.2 fusion.62
  190.7 6.6 all_gather.13
  197.3 7.6 %multiply_reduce_fusion.3 = (f32[]{:T(128)}, f32[1024,1024]{0,1:T(8,128)}) fusion(f32[1024,1024]{0,1:T(8,128)} %copy.7, f32[128,1024]{1,0:T(8,128)S(1)} %all_gather.13, f32[1024,128]{1,0:T(8,128)S(1)} %copy-done), kind=kOutput, calls=%fused_computation.17 | convolution fusion | flops 1613758464 | bytes 9437188 | tf_op jit(solution)/shard_map/dot_general | solution.py:13
  204.9 40.0 %psum.74 = f32[]{:T(128)} all-reduce(f32[]{:T(128)} %get-tuple-element.11), channel_id=1, replica_groups=mesh['pts'=4,'snap'=8] {'pts','snap'}, use_global_device_ids=true, to_apply=%region_11.14 | all-reduce | flops 1 | bytes 8 | tf_op jit(solution)/shard_map/psum | solution.py:18
  245.6 8.5 %fusion.9 = f32[1024,128]{1,0:T(8,128)S(1)} fusion(f32[128,1024]{1,0:T(8,128)S(1)} %all_gather.13, f32[1024,1024]{0,1:T(8,128)} %get-tuple-element.12, f32[]{:T(128)S(6)} %neg.20, f32[]{:T(128)S(6)} %mul.67), kind=kOutput, calls=%fused_computation.14 | convolution fusion | flops 1612709888 | bytes 5242888 | tf_op jit(solution)/shard_map/dot_general | solution.py:13
  254.1 2.5 collective-permute-start
  256.6 10.6 %collective-permute-done = f32[1024,128]{1,0:T(8,128)S(1)} collective-permute-done((f32[1024,128]{1,0:T(8,128)S(1)}, f32[1024,128]{1,0:T(8,128)S(1)}, u32[]{:S(2)}, u32[]{:S(2)}) %collective-permute-start) | collective-permute-done | bytes 524320 | tf_op jit(solution)/shard_map/ppermute | solution.py:48
  267.3 1.6 collective-permute-start.1
  268.8 1.2 fusion.71
  270.5 68.7 %all-reduce.7.cloned.1.call-done = f32[128,128]{0,1:T(8,128)} async-done(((f32[128,128]{0,1:T(8,128)}), f32[128,128]{0,1:T(8,128)}) %all-reduce.7.cloned.1.call-update) | async-done | bytes 65552 | tf_op jit(solution)/shard_map/psum | solution.py:43
  339.2 0.9 select_add_fusion.2
  340.2 1.8 collective-permute-start.2
  342.0 0.9 fusion.60
  342.9 11.7 %cholesky.85 = f32[128,128]{1,0:T(8,128)S(1)} custom-call(f32[128,128]{1,0:T(8,128)S(1)} %fusion.60), custom_call_target="Cholesky" | custom-call | tf_op jit(solution)/shard_map/jit(cholesky)/cholesky | solution.py:44
  355.3 0.7 fusion.45
  355.9 9.8 %custom-call.18 = f32[1,128,128]{1,2,0:T(8,128)S(1)} custom-call(f32[1,128,128]{2,1,0:T(8,128)S(1)} %fusion.45), custom_call_target="InvertDiagBlocksLowerTriangular" | custom-call | tf_op jit(solution)/shard_map/jit(_cho_solve)/triangular_solve | solution.py:49
  367.0 1.2 fusion.72
  368.2 7.6 %multiply_reduce_fusion.2 = (f32[]{:T(128)}, f32[1024,1024]{1,0:T(8,128)}) fusion(f32[1024,1024]{1,0:T(8,128)} %param.8, f32[1024,128]{0,1:T(8,128)S(1)} %fusion.30, f32[128,1024]{1,0:T(8,128)S(1)} %all_gather.13), kind=kOutput, calls=%fused_computation.13 | convolution fusion | flops 1613758464 | bytes 9437188 | tf_op jit(solution)/shard_map/dot_general | solution.py:13
  375.8 40.4 %psum.76 = f32[]{:T(128)} all-reduce(f32[]{:T(128)} %get-tuple-element.13), channel_id=1, replica_groups=mesh['pts'=4,'snap'=8] {'pts','snap'}, use_global_device_ids=true, to_apply=%region_14.18 | all-reduce | flops 1 | bytes 8 | tf_op jit(solution)/shard_map/psum | solution.py:18
  417.0 5.7 fusion.6
  422.7 0.9 select_add_fusion.1
  423.7 0.9 fusion.57
  424.6 11.7 %cholesky.96 = f32[128,128]{1,0:T(8,128)S(1)} custom-call(f32[128,128]{1,0:T(8,128)S(1)} %fusion.57), custom_call_target="Cholesky" | custom-call | tf_op jit(solution)/shard_map/jit(cholesky)/cholesky | solution.py:33
  437.6 9.8 %custom-call.19 = f32[1,128,128]{1,2,0:T(8,128)S(1)} custom-call(f32[1,128,128]{2,1,0:T(8,128)S(1)} %fusion.46), custom_call_target="InvertDiagBlocksLowerTriangular" | custom-call | tf_op jit(solution)/shard_map/jit(_cho_solve)/triangular_solve | solution.py:40
  447.5 1.2 fusion.55
  448.9 8.1 %all_gather.14 = f32[128,1024]{1,0:T(8,128)S(1)} all-gather(f32[128,256]{1,0:T(8,128)S(1)} %convolution_add_fusion.1), channel_id=1, replica_groups=mesh['pts'=4,'snap'=8] {'pts'}, dimensions={1}, use_global_device_ids=true | all-gather | bytes 655360 | tf_op jit(solution)/shard_map/all_gather | solution.py:41
  457.1 7.6 %multiply_reduce_fusion.1 = (f32[]{:T(128)}, f32[1024,1024]{1,0:T(8,128)}) fusion(f32[1024,1024]{1,0:T(8,128)} %param.8, f32[1024,128]{0,1:T(8,128)S(1)} %fusion.30, f32[128,1024]{1,0:T(8,128)S(1)} %all_gather.14), kind=kOutput, calls=%fused_computation.9 | convolution fusion | flops 1613758464 | bytes 9437188 | tf_op jit(solution)/shard_map/dot_general | solution.py:13
  464.7 38.9 %psum.77 = f32[]{:T(128)} all-reduce(f32[]{:T(128)} %get-tuple-element.15), channel_id=1, replica_groups=mesh['pts'=4,'snap'=8] {'pts','snap'}, use_global_device_ids=true, to_apply=%region_17.21 | all-reduce | flops 1 | bytes 8 | tf_op jit(solution)/shard_map/psum | solution.py:18
  504.3 5.7 fusion.3
  510.0 22.0 %reduce-scatter.11.cloned.1.call-done = f32[128,256]{1,0:T(8,128)} async-done(((f32[128,1024]{1,0:T(8,128)}), f32[128,256]{1,0:T(8,128)}) %reduce-scatter.11.cloned.1.call-update) | async-done | bytes 131088 | tf_op jit(solution)/shard_map/reduce_scatter | solution.py:37
  532.0 1.2 fusion.52
  533.5 6.6 all_gather.15
  540.1 7.6 %multiply_reduce_fusion = (f32[]{:T(128)}, f32[1024,1024]{1,0:T(8,128)}) fusion(f32[1024,1024]{1,0:T(8,128)} %param.8, f32[1024,128]{0,1:T(8,128)S(1)} %fusion.30, f32[128,1024]{1,0:T(8,128)S(1)} %all_gather.15), kind=kOutput, calls=%fused_computation.5 | convolution fusion | flops 1613758464 | bytes 9437188 | tf_op jit(solution)/shard_map/dot_general | solution.py:13
  547.6 40.2 %psum.79 = f32[]{:T(128)} all-reduce(f32[]{:T(128)} %get-tuple-element.17), channel_id=1, replica_groups=mesh['pts'=4,'snap'=8] {'pts','snap'}, use_global_device_ids=true, to_apply=%region_21.25 | all-reduce | flops 1 | bytes 8 | tf_op jit(solution)/shard_map/psum | solution.py:18
  588.6 5.2 fusion
  593.8 2.5 collective-permute-start.3
  596.4 10.6 %collective-permute-done.3 = f32[1024,128]{1,0:T(8,128)S(1)} collective-permute-done((f32[1024,128]{1,0:T(8,128)S(1)}, f32[1024,128]{1,0:T(8,128)S(1)}, u32[]{:S(2)}, u32[]{:S(2)}) %collective-permute-start.3) | collective-permute-done | bytes 524320 | tf_op jit(solution)/shard_map/ppermute | solution.py:48
  607.0 1.5 collective-permute-start.4
  608.6 1.2 fusion.73
  609.8 0.8 broadcast_multiply_fusion
  610.6 68.3 %all-reduce.11.cloned.1.call-done = f32[128,128]{0,1:T(8,128)} async-done(((f32[128,128]{0,1:T(8,128)}), f32[128,128]{0,1:T(8,128)}) %all-reduce.11.cloned.1.call-update) | async-done | bytes 65552 | tf_op jit(solution)/shard_map/psum | solution.py:43
  679.0 0.9 select_add_fusion
  680.0 1.8 collective-permute-start.5
  681.8 0.9 fusion.50
  682.6 11.7 %cholesky.107 = f32[128,128]{1,0:T(8,128)S(1)} custom-call(f32[128,128]{1,0:T(8,128)S(1)} %fusion.50), custom_call_target="Cholesky" | custom-call | tf_op jit(solution)/shard_map/jit(cholesky)/cholesky | solution.py:44
  695.7 9.8 %custom-call.21 = f32[1,128,128]{1,2,0:T(8,128)S(1)} custom-call(f32[1,128,128]{2,1,0:T(8,128)S(1)} %fusion.47), custom_call_target="InvertDiagBlocksLowerTriangular" | custom-call | tf_op jit(solution)/shard_map/jit(_cho_solve)/triangular_solve | solution.py:49
  706.7 1.0 copy.16
  (52 shorter events, 9.3 us)
Async XLA Ops:
  7.2 70.4 %all-reduce.5.cloned.1.call-start = ((), (), s32[]{:S(2)}) async-start(), calls=%async_computation.4 | async-start | bytes 131072 | tf_op jit(solution)/shard_map/psum | solution.py:32
  10.1 51.8 %copy-start = (f32[1024,128]{1,0:T(8,128)S(1)}, f32[1024,128]{1,0:T(8,128)}, u32[]{:S(2)}) copy-start(f32[1024,128]{1,0:T(8,128)} %param.9) | copy-start | bytes 1572868
  10.1 92.2 %reduce-scatter.5.cloned.1.call-start = ((), (), s32[]{:S(2)}) async-start(), calls=%async_computation.5 | async-start | bytes 655360 | tf_op jit(solution)/shard_map/reduce_scatter | solution.py:37
  71.6 117.6 %reduce-scatter.7.cloned.1.call-start = ((), (), s32[]{:S(2)}) async-start(), calls=%async_computation.6 | async-start | bytes 655360 | tf_op jit(solution)/shard_map/reduce_scatter | solution.py:37
  167.1 172.1 %all-reduce.7.cloned.1.call-start = ((), (), s32[]{:S(2)}) async-start(), calls=%async_computation.7 | async-start | bytes 131072 | tf_op jit(solution)/shard_map/psum | solution.py:43
  254.1 13.1 %collective-permute-start = (f32[1024,128]{1,0:T(8,128)S(1)}, f32[1024,128]{1,0:T(8,128)S(1)}, u32[]{:S(2)}, u32[]{:S(2)}) collective-permute-start(f32[1024,128]{1,0:T(8,128)S(1)} %fusion.9), channel_id=1, source_target_pairs={{0,1},{1,0},{2,3},{3,2},{4,5},{5,4},{6,7},{7,6},{8,9},{9,8},{10,11... | collective-permute-start | bytes 1572872 | tf_op jit(solution)/shard_map/ppermute | solution.py:48
  267.3 72.9 %collective-permute-start.1 = (f32[1024,128]{1,0:T(8,128)S(1)}, f32[1024,128]{1,0:T(8,128)S(1)}, u32[]{:S(2)}, u32[]{:S(2)}) collective-permute-start(f32[1024,128]{1,0:T(8,128)S(1)} %add.123), channel_id=1, source_target_pairs={{0,2},{1,3},{2,0},{3,1},{4,6},{5,7},{6,4},{7,5},{8,10},{9,11},{10,... | collective-permute-start | bytes 1572872 | tf_op jit(solution)/shard_map/ppermute | solution.py:48
  270.1 152.7 %all-reduce.9.cloned.1.call-start = ((), (), s32[]{:S(2)}) async-start(), calls=%async_computation.8 | async-start | bytes 131072 | tf_op jit(solution)/shard_map/psum | solution.py:32
  340.2 25.5 %collective-permute-start.2 = (f32[1024,128]{1,0:T(8,128)S(1)}, f32[1024,128]{1,0:T(8,128)S(1)}, u32[]{:S(2)}, u32[]{:S(2)}) collective-permute-start(f32[1024,128]{1,0:T(8,128)S(1)} %add.124), channel_id=1, source_target_pairs={{0,4},{1,5},{2,6},{3,7},{4,0},{5,1},{6,2},{7,3},{8,12},{9,13},{10,... | collective-permute-start | bytes 1572872 | tf_op jit(solution)/shard_map/ppermute | solution.py:48
  375.8 71.7 %reduce-scatter.9.cloned.1.call-start = ((), (), s32[]{:S(2)}) async-start(), calls=%async_computation.9 | async-start | bytes 655360 | tf_op jit(solution)/shard_map/reduce_scatter | solution.py:37
  422.7 109.3 %reduce-scatter.11.cloned.1.call-start = ((), (), s32[]{:S(2)}) async-start(), calls=%async_computation.10 | async-start | bytes 655360 | tf_op jit(solution)/shard_map/reduce_scatter | solution.py:37
  510.0 169.0 %all-reduce.11.cloned.1.call-start = ((), (), s32[]{:S(2)}) async-start(), calls=%async_computation.11 | async-start | bytes 131072 | tf_op jit(solution)/shard_map/psum | solution.py:43
  593.8 13.1 %collective-permute-start.3 = (f32[1024,128]{1,0:T(8,128)S(1)}, f32[1024,128]{1,0:T(8,128)S(1)}, u32[]{:S(2)}, u32[]{:S(2)}) collective-permute-start(f32[1024,128]{1,0:T(8,128)S(1)} %fusion), channel_id=1, source_target_pairs={{0,1},{1,0},{2,3},{3,2},{4,5},{5,4},{6,7},{7,6},{8,9},{9,8},{10,11... | collective-permute-start | bytes 1572872 | tf_op jit(solution)/shard_map/ppermute | solution.py:48
  607.0 72.9 %collective-permute-start.4 = (f32[1024,128]{1,0:T(8,128)S(1)}, f32[1024,128]{1,0:T(8,128)S(1)}, u32[]{:S(2)}, u32[]{:S(2)}) collective-permute-start(f32[1024,128]{1,0:T(8,128)S(1)} %add.134), channel_id=1, source_target_pairs={{0,2},{1,3},{2,0},{3,1},{4,6},{5,7},{6,4},{7,5},{8,10},{9,11},{10,... | collective-permute-start | bytes 1572872 | tf_op jit(solution)/shard_map/ppermute | solution.py:48
  680.0 25.5 %collective-permute-start.5 = (f32[1024,128]{1,0:T(8,128)S(1)}, f32[1024,128]{1,0:T(8,128)S(1)}, u32[]{:S(2)}, u32[]{:S(2)}) collective-permute-start(f32[1024,128]{1,0:T(8,128)S(1)} %add.135), channel_id=1, source_target_pairs={{0,4},{1,5},{2,6},{3,7},{4,0},{5,1},{6,2},{7,3},{8,12},{9,13},{10,... | collective-permute-start | bytes 1572872 | tf_op jit(solution)/shard_map/ppermute | solution.py:48
Sparse Core Ops, SparseCore 0:
  10.9 34.2 all-reduce.4
  71.7 21.8 reduce-scatter.4
  167.2 21.8 reduce-scatter.6
  270.2 68.9 all-reduce.6
  375.9 31.3 all-reduce.8
  422.8 21.1 reduce-scatter.8
  510.1 21.8 reduce-scatter.10
  609.9 68.9 all-reduce.10
